TPU v7x, 512 devices: a whole 4x4x16 slice. The times are simulated.
512 devices in a mesh: leaf: 32 (over z_hi, y, core), mat: 16 (over x, z_lo).
Axes of the slice: x: 4, y: 4, z: 16 (z_hi: 4, z_lo: 4; z = z_hi * 4 + z_lo), core: 2. Of those that a mesh axis runs over, the one named last changes fastest.
Arguments:
- leaf_value: float32 [256, 1024, 1024], P('leaf', 'mat'), as said below
- section_cost: float32 [1024, 1024], P('mat'), as said below
- input_cost: float32 [256, 256], replicated, as said below
- dynamics: float32 [1024, 1024], P('mat'), may hold values from -0.1875 to 0.1875
- input_map: float32 [1024, 256], replicated, may hold values from -0.1875 to 0.1875
- parent_of: int32 [256], replicated, may hold values from 0 to 63, as said below
- prob_weight: int32 [256], replicated, may hold values from 1 to 16
- parent_state: float32 [64, 1024], P('leaf', 'mat'), may hold values from -6 to 6
- disturbance: float32 [256, 1024], P('leaf', 'mat'), may hold values from -6 to 6
Outputs:
- parent_value: float32 [64, 1024, 1024], P('leaf', 'mat')
- parent_gain: float32 [64, 1024, 256], P('leaf', 'mat')
- child_state: float32 [256, 1024], P('leaf', 'mat')
Inputs may be any that keep to these rules, and one draw needn't show every extreme that they name: Each leaf_value[l] is symmetric positive definite. `section_cost`: symmetric positive definite. `input_cost`: symmetric positive definite. `parent_of`: every parent has exactly 4 children; the parent of a leaf among the 8 leaves of one leaf index is one of that index's 2 parents, the last parent of the index before, or the first parent of the index after; each leaf index except the ends holds a child of both neighbours' parents.
All inputs are finite; a program needn't handle non-finite values.
Results may differ from a plain program's by a relative error of at most 0.000075.
Values sent between devices are 32-bit elements; how exact they have to be, the bound alone decides.
No kernel may reach another device: no remote copies, remote signals or barrier semaphores. Data moves between devices by JAX's collectives and lax.ppermute only.
A program may use at most 64 MiB of HBM per device.

v0:
```python
import jax
import jax.numpy as jnp
from jax import lax
from jax.experimental import pallas as pl
from jax.experimental.pallas import tpu as pltpu
from jax.sharding import Mesh, PartitionSpec as P

HI = lax.Precision.HIGHEST
LEAF = ("zh", "y", "c")
MAT = ("x", "zl")
BLK = 64


def _panel_step(q, parents, d_ref, cb_ref):
    lane8 = lax.broadcasted_iota(jnp.int32, (8, 128), 0)
    base = pl.multiple_of(q * 8, 8)
    for p in range(parents):
        for c in range(8):
            cb_ref[p, c] = jnp.broadcast_to(d_ref[p, :, c:c + 1], (BLK, 128))
    rows_of = []
    for p in range(parents):
        def element(r, c):
            return jnp.broadcast_to(cb_ref[p, c, pl.ds(base + r, 1), :], (8, 128))

        low = {}
        inv = []
        rows = []
        for c in range(8):
            pivot = element(c, c)
            for t in range(c):
                pivot = pivot - low[c, t] * low[c, t]
            root = lax.rsqrt(pivot)
            root = root * (1.5 - 0.5 * pivot * root * root)
            inv.append(root)
            for r in range(c + 1, 8):
                value = element(r, c)
                for t in range(c):
                    value = value - low[r, t] * low[c, t]
                low[r, c] = value * root
            line = jnp.broadcast_to(d_ref[p, pl.ds(base + c, 1), :], (8, 128))
            for t in range(c):
                line = line - low[c, t] * rows[t]
            rows.append(line * root)
        back = [None] * 8
        for c in range(7, -1, -1):
            line = rows[c]
            for r in range(7, c, -1):
                line = line - low[r, c] * back[r]
            back[c] = line * inv[c]
        block = rows[0]
        for c in range(1, 8):
            block = jnp.where(lane8 == c, rows[c], block)
        rows_of.append((block, back))
    for p in range(parents):
        block, back = rows_of[p]
        for v in range(BLK // 8):
            old = d_ref[p, v * 8:v * 8 + 8, :]
            new = old
            for c in range(8):
                new = new - cb_ref[p, c, v * 8:v * 8 + 8, :] * back[c]
            new = jnp.where(v > q, new, jnp.where(v == q, block, old))
            d_ref[p, v * 8:v * 8 + 8, :] = pltpu.roll(new, 120, 1)


def factor_kernel(h_ref, out_ref, m_ref, d_ref, cb_ref):
    parents, n, _ = h_ref.shape
    row = lax.broadcasted_iota(jnp.int32, (BLK, 128), 0)
    lane = lax.broadcasted_iota(jnp.int32, (BLK, 128), 1)
    unit = jnp.where(lane == row + BLK, 1.0, 0.0)
    full_r = lax.broadcasted_iota(jnp.int32, (n, n), 0)
    full_c = lax.broadcasted_iota(jnp.int32, (n, n), 1)
    for p in range(parents):
        m_ref[p, :, :n] = h_ref[p]
        m_ref[p, :, n:] = jnp.where(full_r == full_c, 1.0, 0.0)
    for k in range(n // BLK):
        top = k * BLK
        lead = (top // 128) * 128
        stop = n + ((top + BLK + 127) // 128) * 128
        for p in range(parents):
            tile = m_ref[p, top:top + BLK, lead:lead + 128]
            if top != lead:
                tile = pltpu.roll(tile, 128 - (top - lead), 1)
            d_ref[p] = jnp.where(lane < BLK, tile, unit)
        lax.fori_loop(0, BLK // 8, lambda q, _: (_panel_step(q, parents, d_ref, cb_ref), 0)[1], 0)
        for p in range(parents):
            inverse = d_ref[p][:, :BLK]
            scaled = jnp.dot(inverse, m_ref[p, top:top + BLK, lead:stop], precision=HI, preferred_element_type=jnp.float32)
            m_ref[p, top:top + BLK, lead:stop] = scaled
            if top + BLK < n:
                left = jnp.transpose(scaled[:, :n - lead])
                left = left[top + BLK - lead:, :]
                m_ref[p, top + BLK:, lead:stop] = m_ref[p, top + BLK:, lead:stop] - jnp.dot(
                    left, scaled, precision=HI, preferred_element_type=jnp.float32)
    for p in range(parents):
        out_ref[p] = m_ref[p, :, n:]


def split(value):
    high = value.astype(jnp.bfloat16)
    return high, (value - high.astype(jnp.float32)).astype(jnp.bfloat16)


def three_pass(left, right, dims=(((1,), (0,)), ((), ()))):
    def part(a, b):
        return lax.dot_general(a, b, dims, preferred_element_type=jnp.float32)

    return part(left[0], right[1]) + part(left[1], right[0]) + part(left[0], right[0])


def exact(left, right, dims=(((1,), (0,)), ((), ()))):
    return lax.dot_general(left, right, dims, precision=HI, preferred_element_type=jnp.float32)


CROSS = (((1,), (1,)), ((), ()))


def piece_of(step, core):
    return jnp.where(step < 4, core * 4 + step, (1 - core) * 4 + step - 4)


def transition_kernel(core_ref, own_ref, other_ref, value_ref, state_ref, turned_ref, high_ref, low_ref, drift_ref, vh_ref, vl_ref, acc_ref):
    step = pl.program_id(0)
    states = value_ref.shape[1]

    @pl.when(step == 0)
    def _():
        vh_ref[...], vl_ref[...] = split(value_ref[...])
        acc_ref[...] = jnp.zeros_like(acc_ref)

    piece = jnp.where(step < 4, own_ref[0, :, :64, :], other_ref[0, :, :64, :]).reshape(states, 128)
    high, low = split(piece)
    high_ref[...] = high
    low_ref[...] = low
    turned_ref[...] = jnp.transpose(three_pass((vh_ref[...], vl_ref[...]), (high, low)))
    for p in range(2):
        acc_ref[p] = acc_ref[p] + piece * state_ref[p : p + 1, :]

    @pl.when(step == 7)
    def _():
        for p in range(2):
            drift_ref[p] = jnp.broadcast_to(jnp.sum(acc_ref[p], axis=1, keepdims=True), (states, 128))


def transition_products(core, own, other, value, state):
    states = value.shape[1]
    rows = own.shape[1:]
    grid = pltpu.PrefetchScalarGridSpec(
        num_scalar_prefetch=1,
        grid=(8,),
        in_specs=[
            pl.BlockSpec((1, *rows), lambda s, c: (jnp.minimum(s, 3), 0, 0, 0)),
            pl.BlockSpec((1, *rows), lambda s, c: (jnp.maximum(s - 4, 0), 0, 0, 0)),
            pl.BlockSpec(value.shape, lambda s, c: (0, 0)),
            pl.BlockSpec((8, 128), lambda s, c: (0, piece_of(s, c[0]))),
        ],
        out_specs=[
            pl.BlockSpec((128, 128), lambda s, c: (piece_of(s, c[0]), 0)),
            pl.BlockSpec((states, 128), lambda s, c: (0, piece_of(s, c[0]))),
            pl.BlockSpec((states, 128), lambda s, c: (0, piece_of(s, c[0]))),
            pl.BlockSpec((2, states, 128), lambda s, c: (0, 0, 0)),
        ],
        scratch_shapes=[
            pltpu.VMEM(value.shape, jnp.bfloat16),
            pltpu.VMEM(value.shape, jnp.bfloat16),
            pltpu.VMEM((2, states, 128), jnp.float32),
        ],
    )
    return pl.pallas_call(
        transition_kernel,
        grid_spec=grid,
        out_shape=[
            jax.ShapeDtypeStruct((states, 128), jnp.float32),
            jax.ShapeDtypeStruct((states, states), jnp.bfloat16),
            jax.ShapeDtypeStruct((states, states), jnp.bfloat16),
            jax.ShapeDtypeStruct((2, states, 128), jnp.float32),
        ],
        cost_estimate=pl.CostEstimate(flops=10**9, bytes_accessed=14 * 10**6, transcendentals=0),
    )(core, own, other, value, state)


def blocks_of(slot_ref, line_refs):
    return [(pl.multiple_of((slot_ref[0] ^ k) * 256, 256), ref) for k, ref in enumerate(line_refs)]


def hessian_kernel(slot_ref, turned_map_ref, cost_ref, drift_ref, line0, line1, line2, line3, out_ref, control_ref, h_ref, m_ref, d_ref, cb_ref):
    n = cost_ref.shape[0]
    parents = out_ref.shape[0]
    total = None
    pull = [jnp.zeros((8, n), jnp.float32) for _ in range(parents)]
    for start, ref in blocks_of(slot_ref, (line0, line1, line2, line3)):
        rows = ref.shape[0]
        term = exact(turned_map_ref[:, pl.ds(start, rows)], ref[...])
        total = term if total is None else total + term
        for p in range(parents):
            weight = drift_ref[p, pl.ds(start, rows), :]
            product = ref[:, p * n : (p + 1) * n] * jnp.concatenate([weight] * (n // 128), axis=1)
            pull[p] = pull[p] + jnp.sum(product.reshape(rows // 8, 8, n), axis=0)
    for p in range(parents):
        h_ref[p] = cost_ref[...] + total[:, p * n : (p + 1) * n]
    factor_kernel(h_ref, out_ref, m_ref, d_ref, cb_ref)
    for p in range(parents):
        coupled = jnp.broadcast_to(jnp.sum(pull[p], axis=0, keepdims=True), (8, n))
        control_ref[p] = -exact(exact(coupled, out_ref[p], CROSS), out_ref[p])


def factor_and_control(slot, turned_map, cost, drift, lines, parents):
    n = cost.shape[0]
    vmem = pl.BlockSpec(memory_space=pltpu.VMEM)
    return pl.pallas_call(
        hessian_kernel,
        in_specs=[pl.BlockSpec(memory_space=pltpu.SMEM)] + [vmem] * 7,
        out_specs=[vmem] * 2,
        out_shape=[
            jax.ShapeDtypeStruct((parents, n, n), jnp.float32),
            jax.ShapeDtypeStruct((parents, 8, n), jnp.float32),
        ],
        scratch_shapes=[
            pltpu.VMEM((parents, n, n), jnp.float32),
            pltpu.VMEM((parents, n, 2 * n), jnp.float32),
            pltpu.VMEM((parents, BLK, 128), jnp.float32),
            pltpu.VMEM((parents, 8, BLK, 128), jnp.float32),
        ],
        cost_estimate=pl.CostEstimate(flops=10**10, bytes_accessed=4 * 10**6, transcendentals=0),
    )(slot, turned_map, cost, drift, *lines)


def value_kernel(slot_ref, arrived_ref, map_ref, inverse_ref, line0, line1, line2, line3, high_ref, low_ref, section_ref, value_ref, gain_ref, cols_ref):
    parents, slab, n = gain_ref.shape
    states = section_ref.shape[1]
    lane = lax.broadcasted_iota(jnp.int32, (slab, 128), 1)
    for i in range(states // 128):
        even, odd = arrived_ref[2 * i], arrived_ref[2 * i + 1]
        cols_ref[:slab, i * 128 : (i + 1) * 128] = jnp.where(lane < 64, even, pltpu.roll(odd, 64, 1))
        cols_ref[slab:, i * 128 : (i + 1) * 128] = jnp.where(lane < 64, pltpu.roll(even, 64, 1), odd)
    coupling = exact(cols_ref[...], map_ref[...])
    for p in range(parents):
        rows = slice(p * slab, (p + 1) * slab)
        gain = -exact(exact(coupling[rows], inverse_ref[p], CROSS), inverse_ref[p])
        gain_ref[p] = gain
        for start, ref in blocks_of(slot_ref, (line0, line1, line2, line3)):
            count = ref.shape[0]
            change = exact(gain, ref[:, p * n : (p + 1) * n], CROSS)
            cols_ref[rows, pl.ds(start, count)] = cols_ref[rows, pl.ds(start, count)] + change
    left = split(cols_ref[...])
    for j in range(states // 256):
        span = slice(j * 256, (j + 1) * 256)
        part = three_pass(left, (high_ref[:, span], low_ref[:, span]))
        for p in range(parents):
            value_ref[p, :, span] = section_ref[:, span] + part[p * slab : (p + 1) * slab]


def value_and_gain(slot, arrived, input_map, inverse, lines, high, low, section):
    parents, n, _ = inverse.shape
    slab, states = section.shape
    vmem = pl.BlockSpec(memory_space=pltpu.VMEM)
    return pl.pallas_call(
        value_kernel,
        in_specs=[pl.BlockSpec(memory_space=pltpu.SMEM)] + [vmem] * 10,
        out_specs=[vmem] * 2,
        out_shape=[
            jax.ShapeDtypeStruct((parents, slab, states), jnp.float32),
            jax.ShapeDtypeStruct((parents, slab, n), jnp.float32),
        ],
        scratch_shapes=[pltpu.VMEM((parents * slab, states), jnp.float32)],
        cost_estimate=pl.CostEstimate(flops=3 * 10**9, bytes_accessed=8 * 10**6, transcendentals=0),
    )(slot, arrived, input_map, inverse, *lines, high, low, section)


def gathered(shard, axis):
    peers = lax.axis_size(axis)
    return lax.all_to_all(jnp.broadcast_to(shard[None], (peers, *shard.shape)), axis, 0, 0, tiled=True)


def sent(value, axis, pairs):
    return lax.ppermute(value, axis, pairs)


def exchanged(shard, axis):
    return [shard] + [sent(shard, axis, [(i, i ^ k) for i in range(4)]) for k in (1, 2, 3)]


def in_order(blocks, place):
    rows = []
    for k in range(4):
        value = blocks[3]
        for distance in (2, 1, 0):
            value = jnp.where(place == (k ^ distance), blocks[distance], value)
        rows.append(value)
    return jnp.concatenate(rows, axis=0)


def neighbours(low_out, high_out):
    count = lax.axis_size(LEAF)
    even = lax.axis_index("c") == 0
    pairs = [(i, i + 1) for i in range(1, count - 1, 2)]
    near = sent(jnp.where(even, high_out, low_out), "c", [(0, 1), (1, 0)])
    far = sent(jnp.where(even, low_out, high_out), LEAF, pairs + [(b, a) for a, b in pairs])
    near, far = lax.optimization_barrier((near, far))
    return jnp.where(even, far, near), jnp.where(even, near, far)


def local(
    leaf_value,
    section_cost,
    input_cost,
    dynamics,
    input_map,
    parent_of,
    prob_weight,
    parent_state,
    disturbance,
):
    leaf_dev, slab, states = leaf_value.shape
    par_dev = parent_state.shape[0]
    inputs = input_map.shape[1]
    leaf_index = lax.axis_index(LEAF)
    column = lax.axis_index(MAT)
    core = lax.axis_index("c")
    slot = lax.axis_index("x").astype(jnp.int32)[None]
    row_start = column * slab

    piece = lax.dynamic_slice_in_dim(dynamics, (core * 4 + lax.axis_index("y")) * 128, 128, 1)
    state_rows = jnp.pad(parent_state, ((0, 8 - par_dev), (0, 128 - slab)))
    from_mat = gathered(jnp.concatenate([piece, state_rows], axis=0), MAT)
    state = jnp.moveaxis(from_mat[:, slab : slab + par_dev, :slab], 0, 1).reshape(par_dev, states)

    weights = prob_weight.astype(jnp.float32)
    my_parents = lax.dynamic_slice_in_dim(parent_of, leaf_index * leaf_dev, leaf_dev, 0)
    my_weights = lax.dynamic_slice_in_dim(weights, leaf_index * leaf_dev, leaf_dev, 0)
    first_label = leaf_index * par_dev
    slot_ids = jnp.arange(par_dev + 2, dtype=jnp.int32)
    chosen = (my_parents - first_label + 1)[:, None] == slot_ids[None, :]
    member = jnp.where(chosen, my_weights[:, None], 0.0)
    labels = first_label + jnp.arange(par_dev, dtype=jnp.int32)
    totals = jnp.sum(
        jnp.where(parent_of[:, None] == labels[None, :], weights[:, None], 0.0), axis=0
    )
    terms = jnp.einsum("st,sij->tij", member, leaf_value, precision=HI)
    mapped = jnp.dot(terms.reshape(-1, states), input_map, precision=HI).reshape(par_dev + 2, slab, inputs)
    map_low, map_high = neighbours(mapped[0], mapped[par_dev + 1])
    from_low, from_high = neighbours(terms[0], terms[par_dev + 1])
    input_side = jnp.concatenate([(mapped[1] + map_low) / totals[0], (mapped[2] + map_high) / totals[1]], axis=1)

    line = in_order(exchanged(input_side, "zl"), lax.axis_index("zl"))
    lines = exchanged(line, "x")

    own_dyn = gathered(from_mat, "y")
    other_dyn = sent(own_dyn, "c", [(0, 1), (1, 0)])
    expected = jnp.concatenate([(terms[1] + from_low) / totals[0], (terms[2] + from_high) / totals[1]], axis=0)
    turned, high, low, drift = transition_products(
        core.astype(jnp.int32)[None], own_dyn, other_dyn, expected, jnp.pad(state, ((0, 8 - par_dev), (0, 0)))
    )
    arrived = lax.all_to_all(turned.reshape(states // slab, slab, par_dev * slab), MAT, 0, 0, tiled=True)
    inverse, control = factor_and_control(slot, input_map.T, input_cost, drift, lines, par_dev)

    input_rows = lax.dynamic_slice_in_dim(input_map, row_start, slab, 0)
    following = jnp.einsum("ij,pj->pi", dynamics, state, precision=HI) + jnp.einsum(
        "ia,pa->pi", input_rows, control[:, 0], precision=HI
    )
    even = core == 0
    near = sent(jnp.where(even, following[par_dev - 1 :], following[:1]), "c", [(0, 1), (1, 0)])
    pairs = [(i, i + 1) for i in range(1, lax.axis_size(LEAF) - 1, 2)]
    far = sent(jnp.where(even, following[:1], following[par_dev - 1 :]), LEAF, pairs + [(b, a) for a, b in pairs])
    new_value, gain_rows = value_and_gain(slot, arrived, input_map, inverse, lines, high, low, section_cost)
    near, far, new_value = lax.optimization_barrier((near, far, new_value))
    extended = jnp.concatenate([jnp.where(even, far, near), following, jnp.where(even, near, far)], axis=0)
    child_state = jnp.einsum("st,tj->sj", chosen.astype(jnp.float32), extended, precision=HI) + disturbance
    return (new_value, gain_rows, child_state)


def solution(mesh):
    fine = Mesh(mesh.devices.reshape(4, 4, 2, 4, 4), (*LEAF, *MAT))
    in_specs = (
        P(LEAF, MAT, None),
        P(MAT, None),
        P(),
        P(MAT, None),
        P(),
        P(),
        P(),
        P(LEAF, MAT),
        P(LEAF, MAT),
    )
    out_specs = (P(LEAF, MAT, None), P(LEAF, MAT, None), P(LEAF, MAT))
    return jax.shard_map(local, mesh=fine, in_specs=in_specs, out_specs=out_specs, check_vma=False)
```

profile of v0, /device:TPU:25, one launch (start us, length us, event | category | flops | bytes accessed | tf_op | source)
XLA Modules:
  0.0 220.3 jit_solution(4452371277401330954)
XLA Ops:
  2.3 25.2 %all_to_all.15 = f32[16,72,128]{2,1,0:T(8,128)S(1)} all-to-all(f32[16,72,128]{2,1,0:T(8,128)S(1)} %broadcast_in_dim.48), channel_id=1, replica_groups=mesh['zh'=4,'y'=4,'c'=2,'x'=4,'zl'=4] {'x','zl'}, dimensions={0} | all-to-all | bytes 1179648 | tf_op jit(solution)/shard_map/all_to_all | solution.py:271
  28.3 1.6 broadcast_in_dim.51
  29.9 4.6 %all-to-all-start.1 = ((f32[4,16,72,128]{3,2,1,0:T(8,128)}), f32[4,16,72,128]{3,2,1,0:T(8,128)}, u32[]{:S(2)}, u32[]{:S(2)}) async-start(f32[4,16,72,128]{3,2,1,0:T(8,128)} %broadcast_in_dim.51), calls=%async_computation.1 | async-start | bytes 4718592 | tf_op jit(solution)/shard_map/all_to_all | solution.py:271
  34.7 25.5 %all-to-all-done.1.own_ref = f32[4,16,72,128]{3,2,1,0:T(8,128)} async-done(((f32[4,16,72,128]{3,2,1,0:T(8,128)}), f32[4,16,72,128]{3,2,1,0:T(8,128)}, u32[]{:S(2)}, u32[]{:S(2)}) %all-to-all-start.1) | async-done | bytes 2359328 | tf_op jit(solution)/shard_map/all_to_all | solution.py:271
  60.2 4.5 %collective-permute-start = (f32[4,16,72,128]{3,2,1,0:T(8,128)}, f32[4,16,72,128]{3,2,1,0:T(8,128)}, u32[]{:S(2)}, u32[]{:S(2)}) collective-permute-start(f32[4,16,72,128]{3,2,1,0:T(8,128)} %all-to-all-done.1.own_ref), channel_id=1, source_target_pairs={{0,16},{16,0},{1,17},{17,1},{2,18},{18,2},{3,19},{19,3},{4,20},{20... | collective-permute-start | bytes 7077896 | tf_op jit(solution)/shard_map/ppermute | solution.py:275
  64.7 3.8 %fusion = f32[4,64,1024]{2,0,1:T(4,128)} fusion(f32[8,64,1024]{2,1,0:T(8,128)S(1)} %copy-done, f32[8]{0:T(128)S(1)} %dynamic_slice.14, s32[8]{0:T(128)S(1)} %subtract_add_fusion), kind=kOutput, calls=%fused_computation | convolution fusion | flops 25165888 | bytes 3145792 | tf_op jit(solution)/shard_map/st,sij->tij/dot_general | solution.py:338
  68.6 1.8 copy.38
  70.4 2.2 %fusion.28 = f32[256,256]{1,0:T(8,128)S(1)} fusion(f32[256,1024]{1,0:T(8,128)S(1)} %bitcast.35, f32[1024,256]{1,0:T(8,128)} %map_ref.1), kind=kOutput, calls=%fused_computation.57 | convolution fusion | flops 805306368 | bytes 2359296 | tf_op jit(solution)/shard_map/dot_general | solution.py:339
  72.7 1.9 collective-permute-start.3
  74.6 10.7 %collective-permute-start.4 = (f32[64,256]{1,0:T(8,128)S(1)}, f32[64,256]{1,0:T(8,128)S(1)}, u32[]{:S(2)}, u32[]{:S(2)}) collective-permute-start(f32[64,256]{1,0:T(8,128)S(1)} %get-tuple-element.43), channel_id=1, source_target_pairs={{16,32},{48,64},{80,96},{112,128},{144,160},{176,192},{208,224},{2... | collective-permute-start | bytes 196616 | tf_op jit(solution)/shard_map/ppermute | solution.py:275
  86.1 3.4 %collective-permute-done.4 = f32[64,256]{1,0:T(8,128)S(1)} collective-permute-done((f32[64,256]{1,0:T(8,128)S(1)}, f32[64,256]{1,0:T(8,128)S(1)}, u32[]{:S(2)}, u32[]{:S(2)}) %collective-permute-start.4) | collective-permute-done | bytes 65568 | tf_op jit(solution)/shard_map/ppermute | solution.py:275
  90.9 1.9 collective-permute-start.5
  92.8 1.9 collective-permute-start.6
  94.7 5.4 %collective-permute-start.7 = (f32[64,512]{1,0:T(8,128)S(1)}, f32[64,512]{1,0:T(8,128)}, u32[]{:S(2)}, u32[]{:S(2)}) collective-permute-start(f32[64,512]{1,0:T(8,128)S(1)} %pad_maximum_fusion.2), channel_id=1, source_target_pairs={{0,3},{1,2},{2,1},{3,0},{4,7},{5,6},{6,5},{7,4},{8,11},{9,10},{10,... | collective-permute-start | bytes 393224 | tf_op jit(solution)/shard_map/ppermute | solution.py:275
  101.0 1.9 collective-permute-start.1
  103.6 8.9 %collective-permute-start.2 = (f32[64,1024]{1,0:T(8,128)}, f32[64,1024]{1,0:T(8,128)}, u32[]{:S(2)}, u32[]{:S(2)}) collective-permute-start(f32[64,1024]{1,0:T(8,128)} %get-tuple-element.35), channel_id=1, source_target_pairs={{16,32},{48,64},{80,96},{112,128},{144,160},{176,192},{208,224},{2... | collective-permute-start | bytes 786440 | tf_op jit(solution)/shard_map/ppermute | solution.py:275
  113.1 1.8 select_select_fusion.3
  115.0 10.3 %collective-permute-done.2 = f32[64,1024]{1,0:T(8,128)} collective-permute-done((f32[64,1024]{1,0:T(8,128)}, f32[64,1024]{1,0:T(8,128)}, u32[]{:S(2)}, u32[]{:S(2)}) %collective-permute-start.2) | collective-permute-done | bytes 262176 | tf_op jit(solution)/shard_map/ppermute | solution.py:275
  125.3 2.3 %fusion.5 = (f32[64,1024]{1,0:T(8,128)S(1)}, f32[64,1024]{1,0:T(8,128)S(1)}) fusion(f32[4,64,1024]{2,1,0:T(8,128)S(1)} %copy.38, f32[64,1024]{1,0:T(8,128)} %collective-permute-done.2, f32[64,1024]{1,0:T(8,128)} %collective-permute-done.1, f32[]{:T(128)} %bitcast.8, pred[]{:T(512)S(6)} %eq.22, f32[]{:T(128)} %bitcast.10), kind=kLoop, calls=%fused_computation.11 | loop fusion | flops 393216 | bytes 1572873 | tf_op jit(solution)/shard_map/div | solution.py:349
  130.0 9.8 %shard_map.112 = (f32[1024,128]{1,0:T(8,128)}, bf16[1024,1024]{1,0:T(8,128)(2,1)}, bf16[1024,1024]{1,0:T(8,128)(2,1)}, f32[2,1024,128]{2,1,0:T(8,128)}) custom-call(s32[1]{0:T(128)} %bitcast.3.core_ref, f32[4,16,72,128]{3,2,1,0:T(8,128)} %all-to-all-done.1.own_ref, f32[4,16,72,128]{3,2,1,0:T(8,128)} %collective-permute-done.other_ref, ...), custom_call_target="tpu_custom_call" | custom-call | flops 1000000000 | bytes 14000000 | tf_op jit(solution)/shard_map/pallas_call | solution.py:168
  139.8 4.4 %all-to-all-start.2 = ((f32[16,64,128]{2,1,0:T(8,128)}), f32[16,64,128]{2,1,0:T(8,128)}, u32[]{:S(2)}, u32[]{:S(2)}) async-start(f32[16,64,128]{2,1,0:T(8,128)} %bitcast.37), calls=%async_computation.2 | async-start | bytes 1048576 | tf_op jit(solution)/shard_map/all_to_all | solution.py:353
  144.2 1.7 pad_maximum_fusion.1.line0
  145.9 3.2 %collective-permute-start.8 = (f32[256,512]{1,0:T(8,128)}, f32[256,512]{1,0:T(8,128)}, u32[]{:S(2)}, u32[]{:S(2)}) collective-permute-start(f32[256,512]{1,0:T(8,128)} %pad_maximum_fusion.1.line0), channel_id=1, source_target_pairs={{0,4},{4,0},{8,12},{12,8},{1,5},{5,1},{9,13},{13,9},{2,6},{6,2},{1... | collective-permute-start | bytes 1572872 | tf_op jit(solution)/shard_map/ppermute | solution.py:275
  149.2 4.4 %collective-permute-start.9 = (f32[256,512]{1,0:T(8,128)}, f32[256,512]{1,0:T(8,128)}, u32[]{:S(2)}, u32[]{:S(2)}) collective-permute-start(f32[256,512]{1,0:T(8,128)} %pad_maximum_fusion.1.line0), channel_id=1, source_target_pairs={{0,8},{4,12},{8,0},{12,4},{1,9},{5,13},{9,1},{13,5},{2,10},{6,14},... | collective-permute-start | bytes 1572872 | tf_op jit(solution)/shard_map/ppermute | solution.py:275
  153.5 2.3 %collective-permute-start.10 = (f32[256,512]{1,0:T(8,128)}, f32[256,512]{1,0:T(8,128)}, u32[]{:S(2)}, u32[]{:S(2)}) collective-permute-start(f32[256,512]{1,0:T(8,128)} %pad_maximum_fusion.1.line0), channel_id=1, source_target_pairs={{0,12},{4,8},{8,4},{12,0},{1,13},{5,9},{9,5},{13,1},{2,14},{6,10},... | collective-permute-start | bytes 1572872 | tf_op jit(solution)/shard_map/ppermute | solution.py:275
  155.9 1.3 copy.36
  158.6 7.5 %collective-permute-done.9.line2 = f32[256,512]{1,0:T(8,128)} collective-permute-done((f32[256,512]{1,0:T(8,128)}, f32[256,512]{1,0:T(8,128)}, u32[]{:S(2)}, u32[]{:S(2)}) %collective-permute-start.9) | collective-permute-done | bytes 524320 | tf_op jit(solution)/shard_map/ppermute | solution.py:275
  166.1 5.5 %collective-permute-done.10.line3 = f32[256,512]{1,0:T(8,128)} collective-permute-done((f32[256,512]{1,0:T(8,128)}, f32[256,512]{1,0:T(8,128)}, u32[]{:S(2)}, u32[]{:S(2)}) %collective-permute-start.10) | collective-permute-done | bytes 524320 | tf_op jit(solution)/shard_map/ppermute | solution.py:275
  171.6 25.7 %shard_map.113 = (f32[2,256,256]{2,1,0:T(8,128)}, f32[2,8,256]{2,1,0:T(8,128)}) custom-call(s32[1]{0:T(128)} %bitcast.1.slot_ref, f32[256,1024]{1,0:T(8,128)} %bitcast.36, f32[256,256]{1,0:T(8,128)} %cost_ref.1, f32[2,1024,128]{2,1,0:T(8,128)} %get-tuple-element.20.drift_ref, f32[256,512]{1,0:T(8,128)} %pad_maximum_fusion.1.line0, ...), custom_call_target="tpu_custom_call" | custom-call | flops 10000000000 | bytes 4000000 | tf_op jit(solution)/shard_map/pallas_call | solution.py:209
  198.2 1.9 collective-permute-start.11
  200.1 9.6 %collective-permute-start.12 = (f32[1,64]{1,0:T(1,128)S(1)}, f32[1,64]{1,0:T(1,128)S(1)}, u32[]{:S(2)}, u32[]{:S(2)}) collective-permute-start(f32[1,64]{1,0:T(1,128)S(1)} %get-tuple-element.47), channel_id=1, source_target_pairs={{16,32},{48,64},{80,96},{112,128},{144,160},{176,192},{208,224},{2... | collective-permute-start | bytes 776 | tf_op jit(solution)/shard_map/ppermute | solution.py:275
  209.7 9.8 %shard_map.114 = (f32[2,64,1024]{2,1,0:T(8,128)}, f32[2,64,256]{2,1,0:T(8,128)}) custom-call(s32[1]{0:T(128)} %bitcast.1.slot_ref, f32[16,64,128]{2,1,0:T(8,128)} %all-to-all-done.2.arrived_ref, f32[1024,256]{1,0:T(8,128)} %map_ref.1, f32[2,256,256]{2,1,0:T(8,128)} %get-tuple-element.25.inverse_ref, f32[256,512]{1,0:T(8,128)} %pad_maximum_fusion.1.line0, ...), custom_call_target="tpu_custom_call" | custom-call | flops 3000000000 | bytes 8000000 | tf_op jit(solution)/shard_map/pallas_call | solution.py:256
  (54 shorter events, 12.4 us)
Async XLA Ops:
  0.6 64.1 %copy-start = (f32[8,64,1024]{2,1,0:T(8,128)S(1)}, f32[8,64,1024]{2,1,0:T(8,128)}, u32[]{:S(2)}) copy-start(f32[8,64,1024]{2,1,0:T(8,128)} %param.9) | copy-start | bytes 6291460
  27.5 0.8 copy-start.2
  29.9 4.7 %copy-start.9 = (s32[256]{0:T(256)S(1)}, s32[256]{0:T(256)}, u32[]{:S(2)}) copy-start(s32[256]{0:T(256)} %param.15) | copy-start | bytes 3076
  29.9 4.8 %copy-start.8 = (s32[256]{0:T(256)S(1)}, s32[256]{0:T(256)}, u32[]{:S(2)}) copy-start(s32[256]{0:T(256)} %param.14) | copy-start | bytes 3076
  29.9 30.3 %all-to-all-start.1 = ((f32[4,16,72,128]{3,2,1,0:T(8,128)}), f32[4,16,72,128]{3,2,1,0:T(8,128)}, u32[]{:S(2)}, u32[]{:S(2)}) async-start(f32[4,16,72,128]{3,2,1,0:T(8,128)} %broadcast_in_dim.51), calls=%async_computation.1 | async-start | bytes 4718592 | tf_op jit(solution)/shard_map/all_to_all | solution.py:271
  60.2 69.8 %collective-permute-start = (f32[4,16,72,128]{3,2,1,0:T(8,128)}, f32[4,16,72,128]{3,2,1,0:T(8,128)}, u32[]{:S(2)}, u32[]{:S(2)}) collective-permute-start(f32[4,16,72,128]{3,2,1,0:T(8,128)} %all-to-all-done.1.own_ref), channel_id=1, source_target_pairs={{0,16},{16,0},{1,17},{17,1},{2,18},{18,2},{3,19},{19,3},{4,20},{20... | collective-permute-start | bytes 7077896 | tf_op jit(solution)/shard_map/ppermute | solution.py:275
  72.7 13.5 %collective-permute-start.3 = (f32[64,256]{1,0:T(8,128)S(1)}, f32[64,256]{1,0:T(8,128)S(1)}, u32[]{:S(2)}, u32[]{:S(2)}) collective-permute-start(f32[64,256]{1,0:T(8,128)S(1)} %get-tuple-element.44), channel_id=1, source_target_pairs={{0,16},{16,0},{1,17},{17,1},{2,18},{18,2},{3,19},{19,3},{4,20},{20... | collective-permute-start | bytes 196616 | tf_op jit(solution)/shard_map/ppermute | solution.py:275
  74.6 15.0 %collective-permute-start.4 = (f32[64,256]{1,0:T(8,128)S(1)}, f32[64,256]{1,0:T(8,128)S(1)}, u32[]{:S(2)}, u32[]{:S(2)}) collective-permute-start(f32[64,256]{1,0:T(8,128)S(1)} %get-tuple-element.43), channel_id=1, source_target_pairs={{16,32},{48,64},{80,96},{112,128},{144,160},{176,192},{208,224},{2... | collective-permute-start | bytes 196616 | tf_op jit(solution)/shard_map/ppermute | solution.py:275
  90.9 12.1 %collective-permute-start.5 = (f32[64,512]{1,0:T(8,128)S(1)}, f32[64,512]{1,0:T(8,128)S(1)}, u32[]{:S(2)}, u32[]{:S(2)}) collective-permute-start(f32[64,512]{1,0:T(8,128)S(1)} %pad_maximum_fusion.2), channel_id=1, source_target_pairs={{0,1},{1,0},{2,3},{3,2},{4,5},{5,4},{6,7},{7,6},{8,9},{9,8},{10,11... | collective-permute-start | bytes 393224 | tf_op jit(solution)/shard_map/ppermute | solution.py:275
  92.8 19.7 %collective-permute-start.6 = (f32[64,512]{1,0:T(8,128)S(1)}, f32[64,512]{1,0:T(8,128)S(1)}, u32[]{:S(2)}, u32[]{:S(2)}) collective-permute-start(f32[64,512]{1,0:T(8,128)S(1)} %pad_maximum_fusion.2), channel_id=1, source_target_pairs={{0,2},{1,3},{2,0},{3,1},{4,6},{5,7},{6,4},{7,5},{8,10},{9,11},{10,... | collective-permute-start | bytes 393224 | tf_op jit(solution)/shard_map/ppermute | solution.py:275
  94.7 18.4 %collective-permute-start.7 = (f32[64,512]{1,0:T(8,128)S(1)}, f32[64,512]{1,0:T(8,128)}, u32[]{:S(2)}, u32[]{:S(2)}) collective-permute-start(f32[64,512]{1,0:T(8,128)S(1)} %pad_maximum_fusion.2), channel_id=1, source_target_pairs={{0,3},{1,2},{2,1},{3,0},{4,7},{5,6},{6,5},{7,4},{8,11},{9,10},{10,... | collective-permute-start | bytes 393224 | tf_op jit(solution)/shard_map/ppermute | solution.py:275
  101.0 14.0 %collective-permute-start.1 = (f32[64,1024]{1,0:T(8,128)}, f32[64,1024]{1,0:T(8,128)}, u32[]{:S(2)}, u32[]{:S(2)}) collective-permute-start(f32[64,1024]{1,0:T(8,128)} %get-tuple-element.36), channel_id=1, source_target_pairs={{0,16},{16,0},{1,17},{17,1},{2,18},{18,2},{3,19},{19,3},{4,20},{20... | collective-permute-start | bytes 786440 | tf_op jit(solution)/shard_map/ppermute | solution.py:275
  102.9 0.7 copy-start.5
  103.6 21.7 %collective-permute-start.2 = (f32[64,1024]{1,0:T(8,128)}, f32[64,1024]{1,0:T(8,128)}, u32[]{:S(2)}, u32[]{:S(2)}) collective-permute-start(f32[64,1024]{1,0:T(8,128)} %get-tuple-element.35), channel_id=1, source_target_pairs={{16,32},{48,64},{80,96},{112,128},{144,160},{176,192},{208,224},{2... | collective-permute-start | bytes 786440 | tf_op jit(solution)/shard_map/ppermute | solution.py:275
  112.5 0.7 copy-start.6
  130.0 14.1 %copy-start.3 = (f32[64,512]{1,0:T(8,128)S(1)}, f32[64,512]{1,0:T(8,128)}, u32[]{:S(2)}) copy-start(f32[64,512]{1,0:T(8,128)} %get-tuple-element.39) | copy-start | bytes 393220
  139.8 16.0 %copy-start.1 = (f32[1024,256]{1,0:T(8,128)S(1)}, f32[1024,256]{1,0:T(8,128)}, u32[]{:S(2)}) copy-start(f32[1024,256]{1,0:T(8,128)} %map_ref.1) | copy-start | bytes 3145732
  139.8 69.9 %all-to-all-start.2 = ((f32[16,64,128]{2,1,0:T(8,128)}), f32[16,64,128]{2,1,0:T(8,128)}, u32[]{:S(2)}, u32[]{:S(2)}) async-start(f32[16,64,128]{2,1,0:T(8,128)} %bitcast.37), calls=%async_computation.2 | async-start | bytes 1048576 | tf_op jit(solution)/shard_map/all_to_all | solution.py:353
  145.9 11.3 %copy-start.4 = (f32[64,1024]{1,0:T(8,128)S(1)}, f32[64,1024]{1,0:T(8,128)}, u32[]{:S(2)}) copy-start(f32[64,1024]{1,0:T(8,128)} %param.12) | copy-start | bytes 786436
  145.9 12.7 %collective-permute-start.8 = (f32[256,512]{1,0:T(8,128)}, f32[256,512]{1,0:T(8,128)}, u32[]{:S(2)}, u32[]{:S(2)}) collective-permute-start(f32[256,512]{1,0:T(8,128)} %pad_maximum_fusion.1.line0), channel_id=1, source_target_pairs={{0,4},{4,0},{8,12},{12,8},{1,5},{5,1},{9,13},{13,9},{2,6},{6,2},{1... | collective-permute-start | bytes 1572872 | tf_op jit(solution)/shard_map/ppermute | solution.py:275
  149.2 16.9 %collective-permute-start.9 = (f32[256,512]{1,0:T(8,128)}, f32[256,512]{1,0:T(8,128)}, u32[]{:S(2)}, u32[]{:S(2)}) collective-permute-start(f32[256,512]{1,0:T(8,128)} %pad_maximum_fusion.1.line0), channel_id=1, source_target_pairs={{0,8},{4,12},{8,0},{12,4},{1,9},{5,13},{9,1},{13,5},{2,10},{6,14},... | collective-permute-start | bytes 1572872 | tf_op jit(solution)/shard_map/ppermute | solution.py:275
  153.5 18.1 %collective-permute-start.10 = (f32[256,512]{1,0:T(8,128)}, f32[256,512]{1,0:T(8,128)}, u32[]{:S(2)}, u32[]{:S(2)}) collective-permute-start(f32[256,512]{1,0:T(8,128)} %pad_maximum_fusion.1.line0), channel_id=1, source_target_pairs={{0,12},{4,8},{8,4},{12,0},{1,13},{5,9},{9,5},{13,1},{2,14},{6,10},... | collective-permute-start | bytes 1572872 | tf_op jit(solution)/shard_map/ppermute | solution.py:275
  198.2 21.3 %collective-permute-start.11 = (f32[1,64]{1,0:T(1,128)S(1)}, f32[1,64]{1,0:T(1,128)S(1)}, u32[]{:S(2)}, u32[]{:S(2)}) collective-permute-start(f32[1,64]{1,0:T(1,128)S(1)} %get-tuple-element.48), channel_id=1, source_target_pairs={{0,16},{16,0},{1,17},{17,1},{2,18},{18,2},{3,19},{19,3},{4,20},{20... | collective-permute-start | bytes 776 | tf_op jit(solution)/shard_map/ppermute | solution.py:275
  200.1 19.4 %collective-permute-start.12 = (f32[1,64]{1,0:T(1,128)S(1)}, f32[1,64]{1,0:T(1,128)S(1)}, u32[]{:S(2)}, u32[]{:S(2)}) collective-permute-start(f32[1,64]{1,0:T(1,128)S(1)} %get-tuple-element.47), channel_id=1, source_target_pairs={{16,32},{48,64},{80,96},{112,128},{144,160},{176,192},{208,224},{2... | collective-permute-start | bytes 776 | tf_op jit(solution)/shard_map/ppermute | solution.py:275
  209.7 9.8 %copy-start.7 = (f32[8,64]{1,0:T(8,128)S(1)}, f32[8,64]{1,0:T(8,128)}, u32[]{:S(2)}) copy-start(f32[8,64]{1,0:T(8,128)} %param.17) | copy-start | bytes 6148
where the time goes:
time: 221 us; the launch traced here: 220 us
  starting transfers between devices  67.6 us (31%)
  waiting for transfers between devices  53.5 us (24%)
  Pallas kernels  45.2 us (20%)
  blocking collectives  25.2 us (11%)
  local copies, waits for them, and re-layouts  10.8 us (5%)
  other arithmetic  9.81 us (4%)
  matrix products  7.29 us (3%)
    ppermute x13, starting transfers between devices, sent(): return lax.ppermute(value, axis, pairs)  58.6 us
    ppermute x13, waiting for transfers between devices, sent(): return lax.ppermute(value, axis, pairs)  28 us
    pallas_call x1, Pallas kernels, factor_and_control(): pl.pallas_call(hessian_kernel, in_specs=[pl.BlockSpec(memory_space=pltpu....  25.7 us
    all_to_all x1, waiting for transfers between devices, gathered(): lax.all_to_all(jnp.broadcast_to(shard[None], (peers, *shard.shape)), axis...  25.5 us
    all_to_all x1, blocking collectives, gathered(): lax.all_to_all(jnp.broadcast_to(shard[None], (peers, *shard.shape)), axis...  25.2 us
    pallas_call x1, Pallas kernels, transition_products(): pl.pallas_call(transition_kernel, grid_spec=grid, out_shape=[jax.ShapeDty...  9.76 us
    pallas_call x1, Pallas kernels, value_and_gain(): pl.pallas_call(value_kernel, in_specs=[pl.BlockSpec(memory_space=pltpu.SM...  9.76 us
    all_to_all x1, starting transfers between devices, gathered(): lax.all_to_all(jnp.broadcast_to(shard[None], (peers, *shard.shape)), axis...  4.62 us
  transfers between devices with their start and end apart: 15, of which 6 were waited for; matrix products, arithmetic and copies ran while one was open for 10% of the time, Pallas kernels for 16%

commit v1 on v0

--- a/solution.py
+++ b/solution.py
@@ -118,27 +118,21 @@
     return jnp.where(step < 4, core * 4 + step, (1 - core) * 4 + step - 4)
 
 
-def transition_kernel(core_ref, own_ref, other_ref, value_ref, state_ref, turned_ref, high_ref, low_ref, drift_ref, vh_ref, vl_ref, acc_ref):
+def transition_kernel(core_ref, own_ref, other_ref, value_ref, state_ref, turned_ref, high_ref, low_ref, drift_ref, vh_ref, vl_ref):
     step = pl.program_id(0)
     states = value_ref.shape[1]
 
     @pl.when(step == 0)
     def _():
         vh_ref[...], vl_ref[...] = split(value_ref[...])
-        acc_ref[...] = jnp.zeros_like(acc_ref)
+        drift_ref[...] = jnp.zeros_like(drift_ref)
 
     piece = jnp.where(step < 4, own_ref[0, :, :64, :], other_ref[0, :, :64, :]).reshape(states, 128)
     high, low = split(piece)
     high_ref[...] = high
     low_ref[...] = low
     turned_ref[...] = jnp.transpose(three_pass((vh_ref[...], vl_ref[...]), (high, low)))
-    for p in range(2):
-        acc_ref[p] = acc_ref[p] + piece * state_ref[p : p + 1, :]
-
-    @pl.when(step == 7)
-    def _():
-        for p in range(2):
-            drift_ref[p] = jnp.broadcast_to(jnp.sum(acc_ref[p], axis=1, keepdims=True), (states, 128))
+    drift_ref[...] += three_pass(split(state_ref[...]), (high, low), CROSS)
 
 
 def transition_products(core, own, other, value, state):
@@ -157,12 +151,11 @@
             pl.BlockSpec((128, 128), lambda s, c: (piece_of(s, c[0]), 0)),
             pl.BlockSpec((states, 128), lambda s, c: (0, piece_of(s, c[0]))),
             pl.BlockSpec((states, 128), lambda s, c: (0, piece_of(s, c[0]))),
-            pl.BlockSpec((2, states, 128), lambda s, c: (0, 0, 0)),
+            pl.BlockSpec((8, states), lambda s, c: (0, 0)),
         ],
         scratch_shapes=[
             pltpu.VMEM(value.shape, jnp.bfloat16),
             pltpu.VMEM(value.shape, jnp.bfloat16),
-            pltpu.VMEM((2, states, 128), jnp.float32),
         ],
     )
     return pl.pallas_call(
@@ -172,7 +165,7 @@
             jax.ShapeDtypeStruct((states, 128), jnp.float32),
             jax.ShapeDtypeStruct((states, states), jnp.bfloat16),
             jax.ShapeDtypeStruct((states, states), jnp.bfloat16),
-            jax.ShapeDtypeStruct((2, states, 128), jnp.float32),
+            jax.ShapeDtypeStruct((8, states), jnp.float32),
         ],
         cost_estimate=pl.CostEstimate(flops=10**9, bytes_accessed=14 * 10**6, transcendentals=0),
     )(core, own, other, value, state)
@@ -186,20 +179,18 @@
     n = cost_ref.shape[0]
     parents = out_ref.shape[0]
     total = None
-    pull = [jnp.zeros((8, n), jnp.float32) for _ in range(parents)]
+    pull = None
     for start, ref in blocks_of(slot_ref, (line0, line1, line2, line3)):
         rows = ref.shape[0]
         term = exact(turned_map_ref[:, pl.ds(start, rows)], ref[...])
         total = term if total is None else total + term
-        for p in range(parents):
-            weight = drift_ref[p, pl.ds(start, rows), :]
-            product = ref[:, p * n : (p + 1) * n] * jnp.concatenate([weight] * (n // 128), axis=1)
-            pull[p] = pull[p] + jnp.sum(product.reshape(rows // 8, 8, n), axis=0)
+        share = exact(drift_ref[:, pl.ds(start, rows)], ref[...])
+        pull = share if pull is None else pull + share
     for p in range(parents):
         h_ref[p] = cost_ref[...] + total[:, p * n : (p + 1) * n]
     factor_kernel(h_ref, out_ref, m_ref, d_ref, cb_ref)
     for p in range(parents):
-        coupled = jnp.broadcast_to(jnp.sum(pull[p], axis=0, keepdims=True), (8, n))
+        coupled = pull[:, p * n : (p + 1) * n]
         control_ref[p] = -exact(exact(coupled, out_ref[p], CROSS), out_ref[p])
 
 
@@ -224,7 +215,10 @@
     )(slot, turned_map, cost, drift, *lines)
 
 
-def value_kernel(slot_ref, arrived_ref, map_ref, inverse_ref, line0, line1, line2, line3, high_ref, low_ref, section_ref, value_ref, gain_ref, cols_ref):
+def value_kernel(slot_ref, arrived_ref, map_ref, inverse_ref, line0, line1, line2, line3, high_hbm, low_hbm, section_ref, value_ref, gain_ref, cols_ref, high_ref, low_ref, sem_ref):
+    copies = [pltpu.make_async_copy(high_hbm, high_ref, sem_ref.at[0]), pltpu.make_async_copy(low_hbm, low_ref, sem_ref.at[1])]
+    for copy in copies:
+        copy.start()
     parents, slab, n = gain_ref.shape
     states = section_ref.shape[1]
     lane = lax.broadcasted_iota(jnp.int32, (slab, 128), 1)
@@ -232,16 +226,18 @@
         even, odd = arrived_ref[2 * i], arrived_ref[2 * i + 1]
         cols_ref[:slab, i * 128 : (i + 1) * 128] = jnp.where(lane < 64, even, pltpu.roll(odd, 64, 1))
         cols_ref[slab:, i * 128 : (i + 1) * 128] = jnp.where(lane < 64, pltpu.roll(even, 64, 1), odd)
-    coupling = exact(cols_ref[...], map_ref[...])
+    coupling = three_pass(split(cols_ref[...]), split(map_ref[...]))
     for p in range(parents):
         rows = slice(p * slab, (p + 1) * slab)
         gain = -exact(exact(coupling[rows], inverse_ref[p], CROSS), inverse_ref[p])
         gain_ref[p] = gain
         for start, ref in blocks_of(slot_ref, (line0, line1, line2, line3)):
             count = ref.shape[0]
-            change = exact(gain, ref[:, p * n : (p + 1) * n], CROSS)
+            change = three_pass(split(gain), split(ref[:, p * n : (p + 1) * n]), CROSS)
             cols_ref[rows, pl.ds(start, count)] = cols_ref[rows, pl.ds(start, count)] + change
     left = split(cols_ref[...])
+    for copy in copies:
+        copy.wait()
     for j in range(states // 256):
         span = slice(j * 256, (j + 1) * 256)
         part = three_pass(left, (high_ref[:, span], low_ref[:, span]))
@@ -255,13 +251,18 @@
     vmem = pl.BlockSpec(memory_space=pltpu.VMEM)
     return pl.pallas_call(
         value_kernel,
-        in_specs=[pl.BlockSpec(memory_space=pltpu.SMEM)] + [vmem] * 10,
+        in_specs=[pl.BlockSpec(memory_space=pltpu.SMEM)] + [vmem] * 7 + [pl.BlockSpec(memory_space=pl.ANY)] * 2 + [vmem],
         out_specs=[vmem] * 2,
         out_shape=[
             jax.ShapeDtypeStruct((parents, slab, states), jnp.float32),
             jax.ShapeDtypeStruct((parents, slab, n), jnp.float32),
         ],
-        scratch_shapes=[pltpu.VMEM((parents * slab, states), jnp.float32)],
+        scratch_shapes=[
+            pltpu.VMEM((parents * slab, states), jnp.float32),
+            pltpu.VMEM((states, states), jnp.bfloat16),
+            pltpu.VMEM((states, states), jnp.bfloat16),
+            pltpu.SemaphoreType.DMA((2,)),
+        ],
         cost_estimate=pl.CostEstimate(flops=3 * 10**9, bytes_accessed=8 * 10**6, transcendentals=0),
     )(slot, arrived, input_map, inverse, *lines, high, low, section)
 
@@ -345,17 +346,22 @@
     lines = exchanged(line, "x")
 
     own_dyn = gathered(from_mat, "y")
+    expected = jnp.concatenate([(terms[1] + from_low) / totals[0], (terms[2] + from_high) / totals[1]], axis=0)
+    padded = jnp.pad(state, ((0, 8 - par_dev), (0, 0)))
+    own_drift = jnp.einsum("ij,pj->pi", dynamics, state, precision=HI)
+    own_dyn, expected, padded, own_drift, turned_map = lax.optimization_barrier(
+        (own_dyn, expected, padded, own_drift, input_map.T)
+    )
     other_dyn = sent(own_dyn, "c", [(0, 1), (1, 0)])
-    expected = jnp.concatenate([(terms[1] + from_low) / totals[0], (terms[2] + from_high) / totals[1]], axis=0)
     turned, high, low, drift = transition_products(
-        core.astype(jnp.int32)[None], own_dyn, other_dyn, expected, jnp.pad(state, ((0, 8 - par_dev), (0, 0)))
+        core.astype(jnp.int32)[None], own_dyn, other_dyn, expected, padded
     )
     arrived = lax.all_to_all(turned.reshape(states // slab, slab, par_dev * slab), MAT, 0, 0, tiled=True)
-    inverse, control = factor_and_control(slot, input_map.T, input_cost, drift, lines, par_dev)
+    inverse, control = factor_and_control(slot, turned_map, input_cost, drift, lines, par_dev)
 
     input_rows = lax.dynamic_slice_in_dim(input_map, row_start, slab, 0)
-    following = jnp.einsum("ij,pj->pi", dynamics, state, precision=HI) + jnp.einsum(
-        "ia,pa->pi", input_rows, control[:, 0], precision=HI
+    following = own_drift + jnp.einsum(
+        "ia,pa->pi", input_rows, jnp.stack([control[p, p] for p in range(par_dev)]), precision=HI
     )
     even = core == 0
     near = sent(jnp.where(even, following[par_dev - 1 :], following[:1]), "c", [(0, 1), (1, 0)])

time: 221 us -> 190 us (0.86)
  blocking collectives: 25.2 us -> 0 us
  waiting for transfers between devices: 53.5 us -> 49 us
  starting transfers between devices: 67.6 us -> 71.8 us
  other arithmetic: 9.81 us -> 6.43 us
    all_to_all x1 -> x0, blocking collectives: 25.2 us -> none  [gathered(): lax.all_to_all(jnp.broadcast_to(shard[None], (peers, *shard.shape)), axis...]
    all_to_all x1 -> x2, waiting for transfers between devices: 25.5 us -> 17.2 us  [gathered(): lax.all_to_all(jnp.broadcast_to(shard[None], (peers, *shard.shape)), axis...]
    all_to_all x1 -> x2, starting transfers between devices: 4.62 us -> 12.8 us  [gathered(): lax.all_to_all(jnp.broadcast_to(shard[None], (peers, *shard.shape)), axis...]
    ppermute x13, waiting for transfers between devices: 28 us -> 31.8 us  [sent(): return lax.ppermute(value, axis, pairs)]
    ppermute x13, starting transfers between devices: 58.6 us -> 54.9 us  [sent(): return lax.ppermute(value, axis, pairs)]
  transfers between devices with their start and end apart: 15 -> 16, of which waited for: 6 -> 7; matrix products, arithmetic and copies ran while one was open for 10% -> 10% of each run, Pallas kernels for 16% -> 23%
where the time goes in v1:
time: 190 us; the launch traced here: 189 us
  starting transfers between devices  71.8 us (38%)
  waiting for transfers between devices  49 us (26%)
  Pallas kernels  43.5 us (23%)
  local copies, waits for them, and re-layouts  10.3 us (5%)
  matrix products  7.1 us (4%)
  other arithmetic  6.43 us (3%)
    ppermute x13, starting transfers between devices, sent(): return lax.ppermute(value, axis, pairs)  54.9 us
    ppermute x13, waiting for transfers between devices, sent(): return lax.ppermute(value, axis, pairs)  31.8 us
    pallas_call x1, Pallas kernels, factor_and_control(): pl.pallas_call(hessian_kernel, in_specs=[pl.BlockSpec(memory_space=pltpu....  26.2 us
    all_to_all x2, waiting for transfers between devices, gathered(): lax.all_to_all(jnp.broadcast_to(shard[None], (peers, *shard.shape)), axis...  17.2 us
    all_to_all x2, starting transfers between devices, gathered(): lax.all_to_all(jnp.broadcast_to(shard[None], (peers, *shard.shape)), axis...  12.8 us
    pallas_call x1, Pallas kernels, value_and_gain(): pl.pallas_call(value_kernel, in_specs=[pl.BlockSpec(memory_space=pltpu.SM...  9.13 us
    pallas_call x1, Pallas kernels, transition_products(): pl.pallas_call(transition_kernel, grid_spec=grid, out_shape=[jax.ShapeDty...  8.25 us
    all_to_all x1, starting transfers between devices, local(): lax.all_to_all(turned.reshape(states // slab, slab, par_dev * slab), MAT,...  4.02 us
  transfers between devices with their start and end apart: 16, of which 7 were waited for; matrix products, arithmetic and copies ran while one was open for 10% of the time, Pallas kernels for 23%

profile of v1, /device:TPU:25, one launch (start us, length us, event | category | flops | bytes accessed | tf_op | source)
XLA Modules:
  0.0 189.2 jit_solution(10162059855787578211)
XLA Ops:
  3.1 8.2 %all-to-all-start = ((f32[16,72,128]{2,1,0:T(8,128)}), f32[16,72,128]{2,1,0:T(8,128)S(1)}, u32[]{:S(2)}, u32[]{:S(2)}) async-start(f32[16,72,128]{2,1,0:T(8,128)} %broadcast_in_dim.48), calls=%async_computation | async-start | bytes 1179648 | tf_op jit(solution)/shard_map/all_to_all | solution.py:272
  11.3 17.2 %all-to-all-done = f32[16,72,128]{2,1,0:T(8,128)S(1)} async-done(((f32[16,72,128]{2,1,0:T(8,128)}), f32[16,72,128]{2,1,0:T(8,128)S(1)}, u32[]{:S(2)}, u32[]{:S(2)}) %all-to-all-start) | async-done | bytes 589856 | tf_op jit(solution)/shard_map/all_to_all | solution.py:272
  28.5 1.6 broadcast_in_dim.49
  30.1 4.6 %all-to-all-start.1 = ((f32[4,16,72,128]{3,2,1,0:T(8,128)}), f32[4,16,72,128]{3,2,1,0:T(8,128)}, u32[]{:S(2)}, u32[]{:S(2)}) async-start(f32[4,16,72,128]{3,2,1,0:T(8,128)} %broadcast_in_dim.49), calls=%async_computation.1 | async-start | bytes 4718592 | tf_op jit(solution)/shard_map/all_to_all | solution.py:272
  34.9 2.8 %fusion = f32[4,64,1024]{2,0,1:T(4,128)S(1)} fusion(f32[8,64,1024]{2,1,0:T(8,128)S(1)} %copy-done, f32[8]{0:T(128)S(1)} %dynamic_slice.14, s32[8]{0:T(128)S(1)} %subtract_add_fusion), kind=kOutput, calls=%fused_computation | convolution fusion | flops 25165888 | bytes 3145792 | tf_op jit(solution)/shard_map/st,sij->tij/dot_general | solution.py:339
  39.2 3.8 %collective-permute-start = (f32[64,1024]{1,0:T(8,128)}, f32[64,1024]{1,0:T(8,128)}, u32[]{:S(2)}, u32[]{:S(2)}) collective-permute-start(f32[64,1024]{1,0:T(8,128)} %get-tuple-element.46), channel_id=1, source_target_pairs={{0,16},{16,0},{1,17},{17,1},{2,18},{18,2},{3,19},{19,3},{4,20},{20... | collective-permute-start | bytes 786440 | tf_op jit(solution)/shard_map/ppermute | solution.py:276
  43.0 8.2 %collective-permute-start.1 = (f32[64,1024]{1,0:T(8,128)}, f32[64,1024]{1,0:T(8,128)}, u32[]{:S(2)}, u32[]{:S(2)}) collective-permute-start(f32[64,1024]{1,0:T(8,128)} %get-tuple-element.45), channel_id=1, source_target_pairs={{16,32},{48,64},{80,96},{112,128},{144,160},{176,192},{208,224},{2... | collective-permute-start | bytes 786440 | tf_op jit(solution)/shard_map/ppermute | solution.py:276
  51.2 2.6 %copy.41 = f32[1024,256]{0,1:T(8,128)} copy(f32[1024,256]{1,0:T(8,128)} %map_ref.1) | data formatting | bytes 2097152 | tf_op args[4]
  54.6 10.7 %collective-permute-done.1 = f32[64,1024]{1,0:T(8,128)} collective-permute-done((f32[64,1024]{1,0:T(8,128)}, f32[64,1024]{1,0:T(8,128)}, u32[]{:S(2)}, u32[]{:S(2)}) %collective-permute-start.1) | collective-permute-done | bytes 262176 | tf_op jit(solution)/shard_map/ppermute | solution.py:276
  65.2 2.4 %fusion.5 = (f32[64,1024]{1,0:T(8,128)S(1)}, f32[64,1024]{1,0:T(8,128)S(1)}) fusion(f32[4,64,1024]{2,1,0:T(8,128)S(1)} %copy.36, f32[64,1024]{1,0:T(8,128)} %collective-permute-done.1, f32[64,1024]{1,0:T(8,128)} %collective-permute-done, f32[]{:T(128)} %bitcast.4, pred[]{:T(512)S(6)} %eq.22, f32[]{:T(128)} %bitcast.6), kind=kLoop, calls=%fused_computation.11 | loop fusion | flops 393216 | bytes 1572873 | tf_op jit(solution)/shard_map/div | solution.py:349
  70.3 2.0 %collective-permute-start.2 = (f32[4,16,72,128]{3,2,1,0:T(8,128)}, f32[4,16,72,128]{3,2,1,0:T(8,128)}, u32[]{:S(2)}, u32[]{:S(2)}) collective-permute-start(f32[4,16,72,128]{3,2,1,0:T(8,128)} %all-to-all-done.1.own_ref), channel_id=1, source_target_pairs={{0,16},{16,0},{1,17},{17,1},{2,18},{18,2},{3,19},{19,3},{4,20},{20... | collective-permute-start | bytes 7077896 | tf_op jit(solution)/shard_map/ppermute | solution.py:276
  72.2 2.2 %fusion.30 = f32[256,256]{1,0:T(8,128)S(1)} fusion(f32[256,1024]{1,0:T(8,128)S(1)} %bitcast.36, f32[1024,256]{1,0:T(8,128)} %map_ref.1), kind=kOutput, calls=%fused_computation.61 | convolution fusion | flops 805306368 | bytes 2359296 | tf_op jit(solution)/shard_map/dot_general | solution.py:340
  74.5 2.4 %collective-permute-start.3 = (f32[64,256]{1,0:T(8,128)S(1)}, f32[64,256]{1,0:T(8,128)S(1)}, u32[]{:S(2)}, u32[]{:S(2)}) collective-permute-start(f32[64,256]{1,0:T(8,128)S(1)} %get-tuple-element.54), channel_id=1, source_target_pairs={{0,16},{16,0},{1,17},{17,1},{2,18},{18,2},{3,19},{19,3},{4,20},{20... | collective-permute-start | bytes 196616 | tf_op jit(solution)/shard_map/ppermute | solution.py:276
  76.9 9.6 %collective-permute-start.4 = (f32[64,256]{1,0:T(8,128)S(1)}, f32[64,256]{1,0:T(8,128)S(1)}, u32[]{:S(2)}, u32[]{:S(2)}) collective-permute-start(f32[64,256]{1,0:T(8,128)S(1)} %get-tuple-element.53), channel_id=1, source_target_pairs={{16,32},{48,64},{80,96},{112,128},{144,160},{176,192},{208,224},{2... | collective-permute-start | bytes 196616 | tf_op jit(solution)/shard_map/ppermute | solution.py:276
  86.5 2.1 %collective-permute-done.4 = f32[64,256]{1,0:T(8,128)S(1)} collective-permute-done((f32[64,256]{1,0:T(8,128)S(1)}, f32[64,256]{1,0:T(8,128)S(1)}, u32[]{:S(2)}, u32[]{:S(2)}) %collective-permute-start.4) | collective-permute-done | bytes 65568 | tf_op jit(solution)/shard_map/ppermute | solution.py:276
  88.6 1.3 fusion.7
  89.9 1.9 %collective-permute-start.5 = (f32[64,512]{1,0:T(8,128)S(1)}, f32[64,512]{1,0:T(8,128)S(1)}, u32[]{:S(2)}, u32[]{:S(2)}) collective-permute-start(f32[64,512]{1,0:T(8,128)S(1)} %pad_maximum_fusion.2), channel_id=1, source_target_pairs={{0,1},{1,0},{2,3},{3,2},{4,5},{5,4},{6,7},{7,6},{8,9},{9,8},{10,11... | collective-permute-start | bytes 393224 | tf_op jit(solution)/shard_map/ppermute | solution.py:276
  91.9 4.2 %collective-permute-start.6 = (f32[64,512]{1,0:T(8,128)S(1)}, f32[64,512]{1,0:T(8,128)S(1)}, u32[]{:S(2)}, u32[]{:S(2)}) collective-permute-start(f32[64,512]{1,0:T(8,128)S(1)} %pad_maximum_fusion.2), channel_id=1, source_target_pairs={{0,2},{1,3},{2,0},{3,1},{4,6},{5,7},{6,4},{7,5},{8,10},{9,11},{10,... | collective-permute-start | bytes 393224 | tf_op jit(solution)/shard_map/ppermute | solution.py:276
  96.1 3.1 %collective-permute-start.7 = (f32[64,512]{1,0:T(8,128)S(1)}, f32[64,512]{1,0:T(8,128)S(1)}, u32[]{:S(2)}, u32[]{:S(2)}) collective-permute-start(f32[64,512]{1,0:T(8,128)S(1)} %pad_maximum_fusion.2), channel_id=1, source_target_pairs={{0,3},{1,2},{2,1},{3,0},{4,7},{5,6},{6,5},{7,4},{8,11},{9,10},{10,... | collective-permute-start | bytes 393224 | tf_op jit(solution)/shard_map/ppermute | solution.py:276
  99.9 3.8 %collective-permute-done.7 = f32[64,512]{1,0:T(8,128)S(1)} collective-permute-done((f32[64,512]{1,0:T(8,128)S(1)}, f32[64,512]{1,0:T(8,128)S(1)}, u32[]{:S(2)}, u32[]{:S(2)}) %collective-permute-start.7) | collective-permute-done | bytes 131104 | tf_op jit(solution)/shard_map/ppermute | solution.py:276
  103.8 2.9 %collective-permute-start.8 = (f32[256,512]{1,0:T(8,128)S(1)}, f32[256,512]{1,0:T(8,128)}, u32[]{:S(2)}, u32[]{:S(2)}) collective-permute-start(f32[256,512]{1,0:T(8,128)S(1)} %pad_maximum_fusion.1.line0), channel_id=1, source_target_pairs={{0,4},{4,0},{8,12},{12,8},{1,5},{5,1},{9,13},{13,9},{2,6},{6,2},{1... | collective-permute-start | bytes 1572872 | tf_op jit(solution)/shard_map/ppermute | solution.py:276
  106.8 4.1 %collective-permute-start.9 = (f32[256,512]{1,0:T(8,128)S(1)}, f32[256,512]{1,0:T(8,128)}, u32[]{:S(2)}, u32[]{:S(2)}) collective-permute-start(f32[256,512]{1,0:T(8,128)S(1)} %pad_maximum_fusion.1.line0), channel_id=1, source_target_pairs={{0,8},{4,12},{8,0},{12,4},{1,9},{5,13},{9,1},{13,5},{2,10},{6,14},... | collective-permute-start | bytes 1572872 | tf_op jit(solution)/shard_map/ppermute | solution.py:276
  110.9 2.6 %collective-permute-start.10 = (f32[256,512]{1,0:T(8,128)S(1)}, f32[256,512]{1,0:T(8,128)}, u32[]{:S(2)}, u32[]{:S(2)}) collective-permute-start(f32[256,512]{1,0:T(8,128)S(1)} %pad_maximum_fusion.1.line0), channel_id=1, source_target_pairs={{0,12},{4,8},{8,4},{12,0},{1,13},{5,9},{9,5},{13,1},{2,14},{6,10},... | collective-permute-start | bytes 1572872 | tf_op jit(solution)/shard_map/ppermute | solution.py:276
  113.4 8.2 %shard_map.112 = (f32[1024,128]{1,0:T(8,128)}, bf16[1024,1024]{1,0:T(8,128)(2,1)}, bf16[1024,1024]{1,0:T(8,128)(2,1)}, f32[8,1024]{1,0:T(8,128)}) custom-call(s32[1]{0:T(128)} %bitcast.10.core_ref, f32[4,16,72,128]{3,2,1,0:T(8,128)} %all-to-all-done.1.own_ref, f32[4,16,72,128]{3,2,1,0:T(8,128)} %collective-permute-done.2.other_ref, ...), custom_call_target="tpu_custom_call" | custom-call | flops 1000000000 | bytes 14000000 | tf_op jit(solution)/shard_map/pallas_call | solution.py:161
  121.7 4.0 %all-to-all-start.2 = ((f32[16,64,128]{2,1,0:T(8,128)}), f32[16,64,128]{2,1,0:T(8,128)S(1)}, u32[]{:S(2)}, u32[]{:S(2)}) async-start(f32[16,64,128]{2,1,0:T(8,128)} %bitcast.38), calls=%async_computation.2 | async-start | bytes 1048576 | tf_op jit(solution)/shard_map/all_to_all | solution.py:359
  125.7 4.4 %collective-permute-done.9.line2 = f32[256,512]{1,0:T(8,128)} collective-permute-done((f32[256,512]{1,0:T(8,128)S(1)}, f32[256,512]{1,0:T(8,128)}, u32[]{:S(2)}, u32[]{:S(2)}) %collective-permute-start.9) | collective-permute-done | bytes 524320 | tf_op jit(solution)/shard_map/ppermute | solution.py:276
  130.1 10.3 %collective-permute-done.10.line3 = f32[256,512]{1,0:T(8,128)} collective-permute-done((f32[256,512]{1,0:T(8,128)S(1)}, f32[256,512]{1,0:T(8,128)}, u32[]{:S(2)}, u32[]{:S(2)}) %collective-permute-start.10) | collective-permute-done | bytes 524320 | tf_op jit(solution)/shard_map/ppermute | solution.py:276
  140.4 26.2 %shard_map.113 = (f32[2,256,256]{2,1,0:T(8,128)}, f32[2,8,256]{2,1,0:T(8,128)}) custom-call(s32[1]{0:T(128)} %bitcast.9.slot_ref, f32[256,1024]{1,0:T(8,128)} %bitcast.37, f32[256,256]{1,0:T(8,128)} %cost_ref.1, f32[8,1024]{1,0:T(8,128)} %get-tuple-element.30.drift_ref, f32[256,512]{1,0:T(8,128)} %copy-done.2, f32[256,512]{1,0:T(8,128)} %collective-permute-done.8.line1, ...), custom_call_target="tpu_custom_call" | custom-call | flops 10000000000 | bytes 4000000 | tf_op jit(solution)/shard_map/pallas_call | solution.py:200
  167.3 1.0 convolution_add_fusion.1
  168.3 1.9 %collective-permute-start.11 = (f32[1,64]{1,0:T(1,128)S(1)}, f32[1,64]{1,0:T(1,128)S(1)}, u32[]{:S(2)}, u32[]{:S(2)}) collective-permute-start(f32[1,64]{1,0:T(1,128)S(1)} %get-tuple-element.60), channel_id=1, source_target_pairs={{0,16},{16,0},{1,17},{17,1},{2,18},{18,2},{3,19},{19,3},{4,20},{20... | collective-permute-start | bytes 776 | tf_op jit(solution)/shard_map/ppermute | solution.py:276
  170.2 8.2 %collective-permute-start.12 = (f32[1,64]{1,0:T(1,128)S(1)}, f32[1,64]{1,0:T(1,128)S(1)}, u32[]{:S(2)}, u32[]{:S(2)}) collective-permute-start(f32[1,64]{1,0:T(1,128)S(1)} %get-tuple-element.59), channel_id=1, source_target_pairs={{16,32},{48,64},{80,96},{112,128},{144,160},{176,192},{208,224},{2... | collective-permute-start | bytes 776 | tf_op jit(solution)/shard_map/ppermute | solution.py:276
  179.2 9.1 %shard_map.114 = (f32[2,64,1024]{2,1,0:T(8,128)}, f32[2,64,256]{2,1,0:T(8,128)}) custom-call(s32[1]{0:T(128)} %bitcast.9.slot_ref, f32[16,64,128]{2,1,0:T(8,128)} %copy-done.3, f32[1024,256]{1,0:T(8,128)} %map_ref.1, f32[2,256,256]{2,1,0:T(8,128)} %get-tuple-element.35.inverse_ref, f32[256,512]{1,0:T(8,128)} %copy-done.2, ...), custom_call_target="tpu_custom_call" | custom-call | flops 3000000000 | bytes 8000000 | tf_op jit(solution)/shard_map/pallas_call | solution.py:252
  (51 shorter events, 10.7 us)
Async XLA Ops:
  0.6 34.3 %copy-start = (f32[8,64,1024]{2,1,0:T(8,128)S(1)}, f32[8,64,1024]{2,1,0:T(8,128)}, u32[]{:S(2)}) copy-start(f32[8,64,1024]{2,1,0:T(8,128)} %param.9) | copy-start | bytes 6291460
  3.1 25.4 %all-to-all-start = ((f32[16,72,128]{2,1,0:T(8,128)}), f32[16,72,128]{2,1,0:T(8,128)S(1)}, u32[]{:S(2)}, u32[]{:S(2)}) async-start(f32[16,72,128]{2,1,0:T(8,128)} %broadcast_in_dim.48), calls=%async_computation | async-start | bytes 1179648 | tf_op jit(solution)/shard_map/all_to_all | solution.py:272
  28.5 1.6 copy-start.1
  30.1 4.6 %copy-start.6 = (s32[256]{0:T(256)S(1)}, s32[256]{0:T(256)}, u32[]{:S(2)}) copy-start(s32[256]{0:T(256)} %param.14) | copy-start | bytes 3076
  30.1 4.7 %copy-start.7 = (s32[256]{0:T(256)S(1)}, s32[256]{0:T(256)}, u32[]{:S(2)}) copy-start(s32[256]{0:T(256)} %param.15) | copy-start | bytes 3076
  30.1 40.2 %all-to-all-start.1 = ((f32[4,16,72,128]{3,2,1,0:T(8,128)}), f32[4,16,72,128]{3,2,1,0:T(8,128)}, u32[]{:S(2)}, u32[]{:S(2)}) async-start(f32[4,16,72,128]{3,2,1,0:T(8,128)} %broadcast_in_dim.49), calls=%async_computation.1 | async-start | bytes 4718592 | tf_op jit(solution)/shard_map/all_to_all | solution.py:272
  39.2 15.4 %collective-permute-start = (f32[64,1024]{1,0:T(8,128)}, f32[64,1024]{1,0:T(8,128)}, u32[]{:S(2)}, u32[]{:S(2)}) collective-permute-start(f32[64,1024]{1,0:T(8,128)} %get-tuple-element.46), channel_id=1, source_target_pairs={{0,16},{16,0},{1,17},{17,1},{2,18},{18,2},{3,19},{19,3},{4,20},{20... | collective-permute-start | bytes 786440 | tf_op jit(solution)/shard_map/ppermute | solution.py:276
  43.0 22.3 %collective-permute-start.1 = (f32[64,1024]{1,0:T(8,128)}, f32[64,1024]{1,0:T(8,128)}, u32[]{:S(2)}, u32[]{:S(2)}) collective-permute-start(f32[64,1024]{1,0:T(8,128)} %get-tuple-element.45), channel_id=1, source_target_pairs={{16,32},{48,64},{80,96},{112,128},{144,160},{176,192},{208,224},{2... | collective-permute-start | bytes 786440 | tf_op jit(solution)/shard_map/ppermute | solution.py:276
  51.2 18.8 %copy-start.4 = (f32[64,1024]{1,0:T(8,128)S(1)}, f32[64,1024]{1,0:T(8,128)}, u32[]{:S(2)}) copy-start(f32[64,1024]{1,0:T(8,128)} %param.12) | copy-start | bytes 786436
  70.3 43.2 %collective-permute-start.2 = (f32[4,16,72,128]{3,2,1,0:T(8,128)}, f32[4,16,72,128]{3,2,1,0:T(8,128)}, u32[]{:S(2)}, u32[]{:S(2)}) collective-permute-start(f32[4,16,72,128]{3,2,1,0:T(8,128)} %all-to-all-done.1.own_ref), channel_id=1, source_target_pairs={{0,16},{16,0},{1,17},{17,1},{2,18},{18,2},{3,19},{19,3},{4,20},{20... | collective-permute-start | bytes 7077896 | tf_op jit(solution)/shard_map/ppermute | solution.py:276
  74.5 12.0 %collective-permute-start.3 = (f32[64,256]{1,0:T(8,128)S(1)}, f32[64,256]{1,0:T(8,128)S(1)}, u32[]{:S(2)}, u32[]{:S(2)}) collective-permute-start(f32[64,256]{1,0:T(8,128)S(1)} %get-tuple-element.54), channel_id=1, source_target_pairs={{0,16},{16,0},{1,17},{17,1},{2,18},{18,2},{3,19},{19,3},{4,20},{20... | collective-permute-start | bytes 196616 | tf_op jit(solution)/shard_map/ppermute | solution.py:276
  76.9 11.7 %collective-permute-start.4 = (f32[64,256]{1,0:T(8,128)S(1)}, f32[64,256]{1,0:T(8,128)S(1)}, u32[]{:S(2)}, u32[]{:S(2)}) collective-permute-start(f32[64,256]{1,0:T(8,128)S(1)} %get-tuple-element.53), channel_id=1, source_target_pairs={{16,32},{48,64},{80,96},{112,128},{144,160},{176,192},{208,224},{2... | collective-permute-start | bytes 196616 | tf_op jit(solution)/shard_map/ppermute | solution.py:276
  89.9 9.3 %collective-permute-start.5 = (f32[64,512]{1,0:T(8,128)S(1)}, f32[64,512]{1,0:T(8,128)S(1)}, u32[]{:S(2)}, u32[]{:S(2)}) collective-permute-start(f32[64,512]{1,0:T(8,128)S(1)} %pad_maximum_fusion.2), channel_id=1, source_target_pairs={{0,1},{1,0},{2,3},{3,2},{4,5},{5,4},{6,7},{7,6},{8,9},{9,8},{10,11... | collective-permute-start | bytes 393224 | tf_op jit(solution)/shard_map/ppermute | solution.py:276
  91.9 8.0 %collective-permute-start.6 = (f32[64,512]{1,0:T(8,128)S(1)}, f32[64,512]{1,0:T(8,128)S(1)}, u32[]{:S(2)}, u32[]{:S(2)}) collective-permute-start(f32[64,512]{1,0:T(8,128)S(1)} %pad_maximum_fusion.2), channel_id=1, source_target_pairs={{0,2},{1,3},{2,0},{3,1},{4,6},{5,7},{6,4},{7,5},{8,10},{9,11},{10,... | collective-permute-start | bytes 393224 | tf_op jit(solution)/shard_map/ppermute | solution.py:276
  96.1 7.6 %collective-permute-start.7 = (f32[64,512]{1,0:T(8,128)S(1)}, f32[64,512]{1,0:T(8,128)S(1)}, u32[]{:S(2)}, u32[]{:S(2)}) collective-permute-start(f32[64,512]{1,0:T(8,128)S(1)} %pad_maximum_fusion.2), channel_id=1, source_target_pairs={{0,3},{1,2},{2,1},{3,0},{4,7},{5,6},{6,5},{7,4},{8,11},{9,10},{10,... | collective-permute-start | bytes 393224 | tf_op jit(solution)/shard_map/ppermute | solution.py:276
  103.8 17.9 %copy-start.2 = (f32[256,512]{1,0:T(8,128)}, f32[256,512]{1,0:T(8,128)S(1)}, u32[]{:S(2)}) copy-start(f32[256,512]{1,0:T(8,128)S(1)} %pad_maximum_fusion.1.line0) | copy-start | bytes 1572868
  103.8 21.9 %collective-permute-start.8 = (f32[256,512]{1,0:T(8,128)S(1)}, f32[256,512]{1,0:T(8,128)}, u32[]{:S(2)}, u32[]{:S(2)}) collective-permute-start(f32[256,512]{1,0:T(8,128)S(1)} %pad_maximum_fusion.1.line0), channel_id=1, source_target_pairs={{0,4},{4,0},{8,12},{12,8},{1,5},{5,1},{9,13},{13,9},{2,6},{6,2},{1... | collective-permute-start | bytes 1572872 | tf_op jit(solution)/shard_map/ppermute | solution.py:276
  106.8 23.4 %collective-permute-start.9 = (f32[256,512]{1,0:T(8,128)S(1)}, f32[256,512]{1,0:T(8,128)}, u32[]{:S(2)}, u32[]{:S(2)}) collective-permute-start(f32[256,512]{1,0:T(8,128)S(1)} %pad_maximum_fusion.1.line0), channel_id=1, source_target_pairs={{0,8},{4,12},{8,0},{12,4},{1,9},{5,13},{9,1},{13,5},{2,10},{6,14},... | collective-permute-start | bytes 1572872 | tf_op jit(solution)/shard_map/ppermute | solution.py:276
  110.9 29.5 %collective-permute-start.10 = (f32[256,512]{1,0:T(8,128)S(1)}, f32[256,512]{1,0:T(8,128)}, u32[]{:S(2)}, u32[]{:S(2)}) collective-permute-start(f32[256,512]{1,0:T(8,128)S(1)} %pad_maximum_fusion.1.line0), channel_id=1, source_target_pairs={{0,12},{4,8},{8,4},{12,0},{1,13},{5,9},{9,5},{13,1},{2,14},{6,10},... | collective-permute-start | bytes 1572872 | tf_op jit(solution)/shard_map/ppermute | solution.py:276
  121.7 56.7 %all-to-all-start.2 = ((f32[16,64,128]{2,1,0:T(8,128)}), f32[16,64,128]{2,1,0:T(8,128)S(1)}, u32[]{:S(2)}, u32[]{:S(2)}) async-start(f32[16,64,128]{2,1,0:T(8,128)} %bitcast.38), calls=%async_computation.2 | async-start | bytes 1048576 | tf_op jit(solution)/shard_map/all_to_all | solution.py:359
  168.3 20.1 %collective-permute-start.11 = (f32[1,64]{1,0:T(1,128)S(1)}, f32[1,64]{1,0:T(1,128)S(1)}, u32[]{:S(2)}, u32[]{:S(2)}) collective-permute-start(f32[1,64]{1,0:T(1,128)S(1)} %get-tuple-element.60), channel_id=1, source_target_pairs={{0,16},{16,0},{1,17},{17,1},{2,18},{18,2},{3,19},{19,3},{4,20},{20... | collective-permute-start | bytes 776 | tf_op jit(solution)/shard_map/ppermute | solution.py:276
  170.2 18.2 %collective-permute-start.12 = (f32[1,64]{1,0:T(1,128)S(1)}, f32[1,64]{1,0:T(1,128)S(1)}, u32[]{:S(2)}, u32[]{:S(2)}) collective-permute-start(f32[1,64]{1,0:T(1,128)S(1)} %get-tuple-element.59), channel_id=1, source_target_pairs={{16,32},{48,64},{80,96},{112,128},{144,160},{176,192},{208,224},{2... | collective-permute-start | bytes 776 | tf_op jit(solution)/shard_map/ppermute | solution.py:276
  178.5 0.8 copy-start.3
  179.2 9.2 %copy-start.5 = (f32[8,64]{1,0:T(8,128)S(1)}, f32[8,64]{1,0:T(8,128)}, u32[]{:S(2)}) copy-start(f32[8,64]{1,0:T(8,128)} %param.17) | copy-start | bytes 6148
